TPU v7x, 32 devices: a whole 2x2x4 slice. The times are simulated.
32 devices in a mesh: grp: 2 (over y), seq: 16 (over z, x, core).
Axes of the slice: x: 2, y: 2, z: 4, core: 2. Of those that a mesh axis runs over, the one named last changes fastest.
Arguments:
- queries: bfloat16 [4096, 128], P(('grp', 'seq')), parts along dimension 0, may hold values from -6 to 6
- keys: bfloat16 [4096, 128], P(('grp', 'seq')), parts along dimension 0, may hold values from -6 to 6
- values: bfloat16 [4096, 128], P(('grp', 'seq')), parts along dimension 0, may hold values from -6 to 6
- log_gate: float32 [4096], P(('grp', 'seq')), parts along dimension 0, may hold values from -1 to 0, as said below
- out_grad: bfloat16 [4096, 128], P(('grp', 'seq')), parts along dimension 0, may hold values from -6 to 6
- segment_order: int32 [64], P(('grp', 'seq')), parts along dimension 0, may hold values from 0 to 31, each once
Outputs:
- attn_out: bfloat16 [4096, 128], P(('grp', 'seq')), parts along dimension 0
- query_grad: float32 [4096, 128], P(('grp', 'seq')), parts along dimension 0
- key_grad: float32 [4096, 128], P(('grp', 'seq')), parts along dimension 0
- value_grad: float32 [4096, 128], P(('grp', 'seq')), parts along dimension 0
- gate_grad: float32 [4096], P(('grp', 'seq')), parts along dimension 0
There are 2 independent parts, one for each index of `grp`. A program takes and returns all parts, laid end to end along the dimension named above; each array names one. Nothing has to cross between parts.
Inputs may be any that keep to these rules, and one draw needn't show every extreme that they name: `log_gate`: every gate is below one. `segment_order`: each segment index appears once.
All inputs are finite; a program needn't handle non-finite values.
Results may differ from a plain program's by a relative error of at most 0.0095.
Values may be sent and summed in bfloat16 or wider, within the bound.
No kernel may reach another device: no remote copies, remote signals or barrier semaphores. Data moves between devices by JAX's collectives and lax.ppermute only.
A program may use at most 64 MiB of HBM per device.

v0:
```python
import jax
import jax.numpy as jnp
from jax import lax
from jax.sharding import PartitionSpec as P

masked_value = -1e30


def contract_last(left, right):
    return lax.dot_general(
        left, right, (((1,), (1,)), ((), ())), preferred_element_type=jnp.float32
    )


def contract_first(left, right):
    return lax.dot_general(
        left, right, (((0,), (0,)), ((), ())), preferred_element_type=jnp.float32
    )


def tile_scores(query_rows, query_gate, query_pos, key_rows, key_gate, key_pos, score_scale):
    scores = (
        contract_last(query_rows, key_rows) * score_scale + query_gate[:, None] - key_gate[None, :]
    )
    visible = key_pos[None, :] <= query_pos[:, None]
    return (scores, visible)


def tile_probs(scores, visible, row_total):
    return jnp.where(visible, jnp.exp(scores - row_total[:, None]), 0.0)


def local(queries, keys, values, log_gate, out_grad, segment_order):
    tokens_here, width = queries.shape
    devices = lax.axis_size("seq")
    segment_rows = tokens_here // 2
    total_len = tokens_here * devices
    score_scale = width ** (-0.5)
    offsets_in = lax.broadcasted_iota(jnp.int32, (1, segment_rows), 1)
    local_cum = jnp.cumsum(log_gate.reshape(2, segment_rows), axis=1)
    segment_total = local_cum[:, -1]
    segment_place = segment_order.astype(jnp.float32)
    own_pos = (segment_order[:, None] * segment_rows + offsets_in).reshape(-1)
    all_totals, all_place = (
        lax.all_gather(segment_total, "seq", axis=0, tiled=True),
        lax.all_gather(segment_place, "seq", axis=0, tiled=True),
    )
    earlier = (all_place[None, :] < segment_place[:, None]).astype(jnp.float32)
    own_offset = jnp.sum(earlier * all_totals[None, :], axis=1)
    own_gate = (local_cum + own_offset[:, None]).reshape(-1)
    all_gate = lax.all_gather(own_gate, "seq", axis=0, tiled=True)
    all_pos = (all_place.astype(jnp.int32)[:, None] * segment_rows + offsets_in).reshape(-1)
    key_all, value_all = (
        lax.all_gather(keys, "seq", axis=0, tiled=True),
        lax.all_gather(values, "seq", axis=0, tiled=True),
    )
    block = 2048
    count = total_len // block

    def key_tile(block_index):
        start = block_index * block
        return (
            lax.dynamic_slice_in_dim(key_all, start, block),
            lax.dynamic_slice_in_dim(value_all, start, block),
            lax.dynamic_slice_in_dim(all_gate, start, block),
            lax.dynamic_slice_in_dim(all_pos, start, block),
        )

    def stats_step(block_index, carry):
        run_max, run_sum = carry
        key_rows, value_rows, key_gate, key_pos = key_tile(block_index)
        scores, visible = tile_scores(
            queries, own_gate, own_pos, key_rows, key_gate, key_pos, score_scale
        )
        kept = jnp.where(visible, scores, masked_value)
        new_max = jnp.maximum(run_max, jnp.max(kept, axis=1))
        fresh = jnp.sum(jnp.where(visible, jnp.exp(kept - new_max[:, None]), 0.0), axis=1)
        return (new_max, run_sum * jnp.exp(run_max - new_max) + fresh)

    start_max = jnp.full((tokens_here,), masked_value, jnp.float32)
    run_max, run_sum = lax.fori_loop(
        0, count, stats_step, (start_max, jnp.zeros((tokens_here,), jnp.float32))
    )
    log_total = run_max + jnp.log(run_sum)

    def output_step(block_index, total):
        key_rows, value_rows, key_gate, key_pos = key_tile(block_index)
        scores, visible = tile_scores(
            queries, own_gate, own_pos, key_rows, key_gate, key_pos, score_scale
        )
        probs = tile_probs(scores, visible, log_total).astype(jnp.bfloat16)
        return total + jnp.dot(probs, value_rows, preferred_element_type=jnp.float32)

    out_full = lax.fori_loop(0, count, output_step, jnp.zeros((tokens_here, width), jnp.float32))
    attn_out = out_full.astype(jnp.bfloat16)
    row_delta = jnp.sum(out_grad.astype(jnp.float32) * out_full, axis=1)

    def row_terms(block_index):
        key_rows, value_rows, key_gate, key_pos = key_tile(block_index)
        scores, visible = tile_scores(
            queries, own_gate, own_pos, key_rows, key_gate, key_pos, score_scale
        )
        probs = tile_probs(scores, visible, log_total)
        dprob = contract_last(out_grad, value_rows)
        return (key_rows, probs, probs * (dprob - row_delta[:, None]))

    def query_step(block_index, total):
        key_rows, probs, dscore = row_terms(block_index)
        return total + jnp.dot(
            dscore.astype(jnp.bfloat16), key_rows, preferred_element_type=jnp.float32
        )

    query_acc = lax.fori_loop(0, count, query_step, jnp.zeros((tokens_here, width), jnp.float32))
    query_all, grad_all = (
        lax.all_gather(queries, "seq", axis=0, tiled=True),
        lax.all_gather(out_grad, "seq", axis=0, tiled=True),
    )
    total_all, delta_all = (
        lax.all_gather(log_total, "seq", axis=0, tiled=True),
        lax.all_gather(row_delta, "seq", axis=0, tiled=True),
    )

    def column_step(block_index, carry):
        key_acc, value_acc, column_acc = carry
        start = block_index * block
        query_rows = lax.dynamic_slice_in_dim(query_all, start, block)
        grad_rows = lax.dynamic_slice_in_dim(grad_all, start, block)
        scores, visible = tile_scores(
            query_rows,
            lax.dynamic_slice_in_dim(all_gate, start, block),
            lax.dynamic_slice_in_dim(all_pos, start, block),
            keys,
            own_gate,
            own_pos,
            score_scale,
        )
        probs = tile_probs(scores, visible, lax.dynamic_slice_in_dim(total_all, start, block))
        dprob = contract_last(grad_rows, values)
        dscore = probs * (dprob - lax.dynamic_slice_in_dim(delta_all, start, block)[:, None])
        dscore_low = dscore.astype(jnp.bfloat16)
        key_acc = key_acc + contract_first(dscore_low, query_rows) * score_scale
        value_acc = value_acc + contract_first(probs.astype(jnp.bfloat16), grad_rows)
        column_acc = column_acc - jnp.sum(dscore, axis=0)
        return (key_acc, value_acc, column_acc)

    zeros_own = jnp.zeros((tokens_here, width), jnp.float32)
    key_grad, value_grad, gate_point = lax.fori_loop(
        0, count, column_step, (zeros_own, zeros_own, jnp.zeros((tokens_here,), jnp.float32))
    )
    query_grad = query_acc * score_scale
    point_rows = gate_point.reshape(2, segment_rows)
    within = jnp.flip(jnp.cumsum(jnp.flip(point_rows, 1), axis=1), 1)
    all_point = lax.all_gather(within[:, 0], "seq", axis=0, tiled=True)
    later = (all_place[None, :] > segment_place[:, None]).astype(jnp.float32)
    gate_grad = (within + jnp.sum(later * all_point[None, :], axis=1)[:, None]).reshape(-1)
    return (attn_out, query_grad, key_grad, value_grad, gate_grad)


def solution(mesh):
    placed = (
        P(("grp", "seq"), None),
        P(("grp", "seq"), None),
        P(("grp", "seq"), None),
        P(("grp", "seq")),
        P(("grp", "seq"), None),
        P(("grp", "seq")),
    )
    return jax.shard_map(
        local,
        mesh=mesh,
        in_specs=placed,
        out_specs=(
            P(("grp", "seq"), None),
            P(("grp", "seq"), None),
            P(("grp", "seq"), None),
            P(("grp", "seq"), None),
            P(("grp", "seq")),
        ),
        check_vma=False,
    )
```

profile of v0, /device:TPU:0, one launch (start us, length us, event | category | flops | bytes accessed | tf_op | source)
XLA Modules:
  0.0 211.5 jit_solution(15644140626693972713)
XLA Ops:
  0.6 0.0 copy-start
  0.6 0.9 copy.17
  1.5 0.0 copy-start.4
  1.5 24.6 %all_gather.34 = bf16[2048,128]{1,0:T(8,128)(2,1)S(1)} all-gather(bf16[128,128]{1,0:T(8,128)(2,1)S(1)} %copy-done), channel_id=1, replica_groups=mesh['grp'=2,'seq'=16] {'seq'}, dimensions={0}, use_global_device_ids=true | all-gather | bytes 557056 | tf_op jit(solution)/shard_map/all_gather | solution.py:55
  26.2 0.1 reshape.129
  26.2 0.2 reduce_window_sum.17
  26.5 0.2 slice_reduce_fusion.1
  26.7 0.6 copy-done.6
  27.3 0.6 dynamic-slice
  28.6 0.2 dynamic-update-slice.1
  28.8 0.7 copy-done.5
  29.5 0.1 convert_dynamic-update-slice_fusion
  29.5 29.8 %all-reduce.3 = (f32[32]{0:T(128)S(1)}, f32[32]{0:T(128)S(1)}) all-reduce(f32[32]{0:T(128)S(1)} %dynamic-update-slice.1, f32[32]{0:T(128)S(1)} %convert_dynamic-update-slice_fusion), channel_id=2, replica_groups=mesh['grp'=2,'seq'=16] {'seq'}, use_global_device_ids=true, to_apply=%add.1 | all-reduce | flops 64 | bytes 512
  59.4 0.1 iota_add_fusion
  59.4 0.1 add.179
  59.5 0.1 iota_add_fusion.1
  59.6 0.1 add.183
  59.7 0.2 fusion.29
  59.9 0.1 broadcast_add_fusion.1
  59.9 0.1 reshape.142
  60.0 17.1 %all-gather.2 = f32[16,1,128]{2,1,0:T(1,128)S(1)} all-gather(f32[1,1,128]{2,1,0:T(1,128)S(1)} %reshape.142), channel_id=1, replica_groups=mesh['grp'=2,'seq'=16] {'seq'}, dimensions={0}, use_global_device_ids=true | all-gather | bytes 8704 | tf_op jit(solution)/shard_map/all_gather | solution.py:51
  77.2 0.1 add.186
  77.2 20.7 %all_gather.31 = bf16[2048,128]{1,0:T(8,128)(2,1)S(1)} all-gather(bf16[128,128]{1,0:T(8,128)(2,1)S(1)} %copy-done.3), channel_id=1, replica_groups=mesh['grp'=2,'seq'=16] {'seq'}, dimensions={0}, use_global_device_ids=true | all-gather | bytes 557056 | tf_op jit(solution)/shard_map/all_gather | solution.py:54
  98.0 0.0 copy-done.2
  98.0 0.5 fusion.13
  98.4 0.4 fusion.12
  98.8 0.5 multiply_reduce_fusion
  99.3 0.7 copy.18
  100.0 0.0 copy-done.1
  100.1 1.2 fusion.11
  101.3 18.9 %all_gather.35 = bf16[2048,128]{1,0:T(8,128)(2,1)S(1)} all-gather(bf16[128,128]{1,0:T(8,128)(2,1)S(1)} %copy-done.2), channel_id=1, replica_groups=mesh['grp'=2,'seq'=16] {'seq'}, dimensions={0}, use_global_device_ids=true | all-gather | bytes 557056 | tf_op jit(solution)/shard_map/all_gather | solution.py:115
  120.1 18.8 %all-gather.3 = f32[16,1,128]{2,1,0:T(1,128)S(1)} all-gather(f32[1,1,128]{2,1,0:T(1,128)S(1)} %bitcast.24), channel_id=1, replica_groups=mesh['grp'=2,'seq'=16] {'seq'}, dimensions={0}, use_global_device_ids=true | all-gather | bytes 8704 | tf_op jit(solution)/shard_map/all_gather | solution.py:119
  138.9 0.9 fusion.5
  139.8 17.4 %all-gather.4 = f32[16,1,128]{2,1,0:T(1,128)S(1)} all-gather(f32[1,1,128]{2,1,0:T(1,128)S(1)} %bitcast.23), channel_id=1, replica_groups=mesh['grp'=2,'seq'=16] {'seq'}, dimensions={0}, use_global_device_ids=true | all-gather | bytes 8704 | tf_op jit(solution)/shard_map/all_gather | solution.py:120
  157.2 20.3 %all_gather.37 = bf16[2048,128]{1,0:T(8,128)(2,1)S(1)} all-gather(bf16[128,128]{1,0:T(8,128)(2,1)S(1)} %copy-done.1), channel_id=1, replica_groups=mesh['grp'=2,'seq'=16] {'seq'}, dimensions={0}, use_global_device_ids=true | all-gather | bytes 557056 | tf_op jit(solution)/shard_map/all_gather | solution.py:116
  177.5 0.4 fusion.33
  178.0 1.0 convolution_multiply_fusion.2
  178.9 1.0 fusion.17
  179.9 0.1 reduce_sum.53
  180.0 0.1 reverse.4
  180.1 0.2 reduce_window_sum.18
  180.3 0.1 rev.8
  180.4 0.2 slice_reduce_fusion
  180.6 0.2 dynamic-update-slice.2
  180.9 29.8 %all-reduce.2 = f32[32]{0:T(128)S(1)} all-reduce(f32[32]{0:T(128)S(1)} %dynamic-update-slice.2), channel_id=3, replica_groups=mesh['grp'=2,'seq'=16] {'seq'}, use_global_device_ids=true, to_apply=%add.2 | all-reduce | flops 32 | bytes 256
  210.7 0.2 fusion.30
  210.9 0.1 broadcast_add_fusion
  210.9 0.6 reshape.130
  (16 shorter events, 0.1 us)
Async XLA Ops:
  0.6 0.9 copy-start
  1.5 24.6 %copy-start.4 = (f32[128]{0:T(128)S(1)}, f32[128]{0:T(128)}, u32[]{:S(2)}) copy-start(f32[128]{0:T(128)} %param.9) | copy-start | bytes 1540
  26.7 0.7 copy-start.6
  28.8 0.7 copy-start.5
  59.4 17.9 %copy-start.3 = (bf16[128,128]{1,0:T(8,128)(2,1)S(1)}, bf16[128,128]{1,0:T(8,128)(2,1)}, u32[]{:S(2)}) copy-start(bf16[128,128]{1,0:T(8,128)(2,1)} %param.7) | copy-start | bytes 98308
  77.2 20.7 %copy-start.2 = (bf16[128,128]{1,0:T(8,128)(2,1)S(1)}, bf16[128,128]{1,0:T(8,128)(2,1)}, u32[]{:S(2)}) copy-start(bf16[128,128]{1,0:T(8,128)(2,1)} %param.6) | copy-start | bytes 98308
  99.3 0.8 copy-start.1
where the time goes:
time: 212 us
  blocking collectives  197 us (93%)
  local copies, waits for them, and re-layouts  5.65 us (3%)
  matrix products  5.38 us (3%)
    unnamed x2, blocking collectives  59.6 us
    all_gather x1, blocking collectives, local(): lax.all_gather(values, 'seq', axis=0, tiled=True)  24.6 us
    all_gather x1, blocking collectives, local(): lax.all_gather(keys, 'seq', axis=0, tiled=True)  20.7 us
    all_gather x1, blocking collectives, local(): lax.all_gather(out_grad, 'seq', axis=0, tiled=True)  20.3 us
    all_gather x1, blocking collectives, local(): lax.all_gather(queries, 'seq', axis=0, tiled=True)  18.9 us
    all_gather x1, blocking collectives, local(): lax.all_gather(log_total, 'seq', axis=0, tiled=True)  18.8 us
    all_gather x1, blocking collectives, local(): lax.all_gather(row_delta, 'seq', axis=0, tiled=True)  17.4 us
    all_gather x1, blocking collectives, local(): all_gate = lax.all_gather(own_gate, 'seq', axis=0, tiled=True)  17.1 us

commit v1 on v0

--- a/solution.py
+++ b/solution.py
@@ -2,6 +2,7 @@
 import jax.numpy as jnp
 from jax import lax
 from jax.sharding import PartitionSpec as P
+from jax.lax import axis_index, axis_size, ppermute
 
 masked_value = -1e30
 
@@ -31,6 +32,23 @@
 
 
 def local(queries, keys, values, log_gate, out_grad, segment_order):
+
+    def work_flows_on_mesh(base_x, mesh_dim):
+        slots = axis_size(mesh_dim)
+        prior = map(lambda idx: (idx - 1, idx), range(1, slots))
+        right_arr = list(prior)
+        tall = right_arr + [(slots - 1, 0)]
+        parts_out = base_x
+        by_rank = [parts_out]
+        for _ in range(slots - 1):
+            parts_out = ppermute(parts_out, mesh_dim, tall)
+            by_rank += [parts_out]
+        return jnp.roll(
+            jnp.concatenate([*reversed(by_rank)], 0),
+            (axis_index(mesh_dim) + 1) * parts_out.shape[0],
+            0,
+        )
+
     tokens_here, width = queries.shape
     devices = lax.axis_size("seq")
     segment_rows = tokens_here // 2
@@ -48,7 +66,7 @@
     earlier = (all_place[None, :] < segment_place[:, None]).astype(jnp.float32)
     own_offset = jnp.sum(earlier * all_totals[None, :], axis=1)
     own_gate = (local_cum + own_offset[:, None]).reshape(-1)
-    all_gate = lax.all_gather(own_gate, "seq", axis=0, tiled=True)
+    all_gate = work_flows_on_mesh(own_gate, "seq")
     all_pos = (all_place.astype(jnp.int32)[:, None] * segment_rows + offsets_in).reshape(-1)
     key_all, value_all = (
         lax.all_gather(keys, "seq", axis=0, tiled=True),

time: 212 us -> 264 us (1.25)
  waiting for transfers between devices: 0 us -> 61.5 us
  blocking collectives: 197 us -> 182 us
  matrix products: 5.38 us -> 9.15 us
    ppermute x0 -> x15, waiting for transfers between devices: none -> 61.5 us  [work_flows_on_mesh(): parts_out = ppermute(parts_out, mesh_dim, tall)]
    all_gather x1 -> x0, blocking collectives: 17.1 us -> none  [local(): all_gate = lax.all_gather(own_gate, 'seq', axis=0, tiled=True)]
    unnamed x2, blocking collectives: 59.6 us -> 64.7 us
    all_gather x1, blocking collectives: 24.6 us -> 21.8 us  [local(): lax.all_gather(values, 'seq', axis=0, tiled=True)]
  transfers between devices with their start and end apart: 0 -> 15, of which waited for: 0 -> 11; matrix products, arithmetic and copies ran while one was open for 0% -> 0% of each run, Pallas kernels for 0% -> 0%
where the time goes in v1:
time: 264 us; the launch traced here: 263 us
  blocking collectives  182 us (69%)
  waiting for transfers between devices  61.5 us (23%)
  matrix products  9.15 us (3%)
  local copies, waits for them, and re-layouts  4.94 us (2%)
  other arithmetic  3.09 us (1%)
    unnamed x2, blocking collectives  64.7 us
    ppermute x15, waiting for transfers between devices, work_flows_on_mesh(): parts_out = ppermute(parts_out, mesh_dim, tall)  61.5 us
    all_gather x1, blocking collectives, local(): lax.all_gather(values, 'seq', axis=0, tiled=True)  21.8 us
    all_gather x1, blocking collectives, local(): lax.all_gather(out_grad, 'seq', axis=0, tiled=True)  20.5 us
    all_gather x1, blocking collectives, local(): lax.all_gather(queries, 'seq', axis=0, tiled=True)  19.4 us
    all_gather x1, blocking collectives, local(): lax.all_gather(keys, 'seq', axis=0, tiled=True)  19.4 us
    all_gather x1, blocking collectives, local(): lax.all_gather(log_total, 'seq', axis=0, tiled=True)  19.1 us
    all_gather x1, blocking collectives, local(): lax.all_gather(row_delta, 'seq', axis=0, tiled=True)  17.1 us
  transfers between devices with their start and end apart: 15, of which 11 were waited for; matrix products, arithmetic and copies ran while one was open for 0% of the time, Pallas kernels for 0%

profile of v1, /device:TPU:0, one launch (start us, length us, event | category | flops | bytes accessed | tf_op | source)
XLA Modules:
  0.0 263.2 jit_solution(4911089004829261858)
XLA Ops:
  0.7 0.7 reshape.129
  1.4 0.2 reduce_window_sum.17
  1.6 0.2 slice_reduce_fusion.1
  1.8 0.7 broadcast_multiply_fusion
  2.6 0.6 dynamic-slice
  3.8 0.8 convert_dynamic-update-slice_fusion
  4.6 0.2 dynamic-update-slice.1
  4.8 34.9 %all-reduce.3 = (f32[32]{0:T(128)S(1)}, f32[32]{0:T(128)S(1)}) all-reduce(f32[32]{0:T(128)S(1)} %dynamic-update-slice.1, f32[32]{0:T(128)S(1)} %convert_dynamic-update-slice_fusion), channel_id=2, replica_groups=mesh['grp'=2,'seq'=16] {'seq'}, use_global_device_ids=true, to_apply=%add.1 | all-reduce | flops 64 | bytes 512
  39.7 0.2 fusion.21
  40.0 5.7 %collective-permute-done = f32[128]{0:T(128)S(1)} collective-permute-done((f32[128]{0:T(128)S(1)}, f32[128]{0:T(128)S(1)}, u32[]{:S(2)}, u32[]{:S(2)}) %collective-permute-start) | collective-permute-done | bytes 544 | tf_op jit(solution)/shard_map/ppermute | solution.py:44
  45.7 5.7 %collective-permute-done.1 = f32[128]{0:T(128)S(1)} collective-permute-done((f32[128]{0:T(128)S(1)}, f32[128]{0:T(128)S(1)}, u32[]{:S(2)}, u32[]{:S(2)}) %collective-permute-start.1) | collective-permute-done | bytes 544 | tf_op jit(solution)/shard_map/ppermute | solution.py:44
  51.4 5.7 %collective-permute-done.2 = f32[128]{0:T(128)S(1)} collective-permute-done((f32[128]{0:T(128)S(1)}, f32[128]{0:T(128)S(1)}, u32[]{:S(2)}, u32[]{:S(2)}) %collective-permute-start.2) | collective-permute-done | bytes 544 | tf_op jit(solution)/shard_map/ppermute | solution.py:44
  57.1 5.7 %collective-permute-done.3 = f32[128]{0:T(128)S(1)} collective-permute-done((f32[128]{0:T(128)S(1)}, f32[128]{0:T(128)S(1)}, u32[]{:S(2)}, u32[]{:S(2)}) %collective-permute-start.3) | collective-permute-done | bytes 544 | tf_op jit(solution)/shard_map/ppermute | solution.py:44
  62.8 19.4 %all_gather.31 = bf16[2048,128]{1,0:T(8,128)(2,1)S(1)} all-gather(bf16[128,128]{1,0:T(8,128)(2,1)S(1)} %copy-done.4), channel_id=1, replica_groups=mesh['grp'=2,'seq'=16] {'seq'}, dimensions={0}, use_global_device_ids=true | all-gather | bytes 557056 | tf_op jit(solution)/shard_map/all_gather | solution.py:133
  82.2 0.2 collective-permute-start.5
  82.4 0.3 convolution_multiply_fusion
  82.7 5.2 %collective-permute-done.5 = f32[128]{0:T(128)S(1)} collective-permute-done((f32[128]{0:T(128)S(1)}, f32[128]{0:T(128)S(1)}, u32[]{:S(2)}, u32[]{:S(2)}) %collective-permute-start.5) | collective-permute-done | bytes 544 | tf_op jit(solution)/shard_map/ppermute | solution.py:44
  87.9 19.4 %all_gather.28 = bf16[2048,128]{1,0:T(8,128)(2,1)S(1)} all-gather(bf16[128,128]{1,0:T(8,128)(2,1)S(1)} %copy-done.2), channel_id=1, replica_groups=mesh['grp'=2,'seq'=16] {'seq'}, dimensions={0}, use_global_device_ids=true | all-gather | bytes 557056 | tf_op jit(solution)/shard_map/all_gather | solution.py:72
  107.3 0.2 collective-permute-start.7
  107.5 21.8 %all_gather.30 = bf16[2048,128]{1,0:T(8,128)(2,1)} all-gather(bf16[128,128]{1,0:T(8,128)(2,1)S(1)} %copy-done.5), channel_id=1, replica_groups=mesh['grp'=2,'seq'=16] {'seq'}, dimensions={0}, use_global_device_ids=true | all-gather | bytes 557056 | tf_op jit(solution)/shard_map/all_gather | solution.py:73
  129.3 0.3 collective-permute-start.8
  129.6 20.5 %all_gather.33 = bf16[2048,128]{1,0:T(8,128)(2,1)} all-gather(bf16[128,128]{1,0:T(8,128)(2,1)S(1)} %copy-done.3), channel_id=1, replica_groups=mesh['grp'=2,'seq'=16] {'seq'}, dimensions={0}, use_global_device_ids=true | all-gather | bytes 557056 | tf_op jit(solution)/shard_map/all_gather | solution.py:134
  150.1 0.2 collective-permute-start.9
  150.3 5.5 %collective-permute-done.9 = f32[128]{0:T(128)S(1)} collective-permute-done((f32[128]{0:T(128)S(1)}, f32[128]{0:T(128)S(1)}, u32[]{:S(2)}, u32[]{:S(2)}) %collective-permute-start.9) | collective-permute-done | bytes 544 | tf_op jit(solution)/shard_map/ppermute | solution.py:44
  155.9 5.6 %collective-permute-done.10 = f32[128]{0:T(128)S(1)} collective-permute-done((f32[128]{0:T(128)S(1)}, f32[128]{0:T(128)S(1)}, u32[]{:S(2)}, u32[]{:S(2)}) %collective-permute-start.10) | collective-permute-done | bytes 544 | tf_op jit(solution)/shard_map/ppermute | solution.py:44
  161.6 5.6 %collective-permute-done.11 = f32[128]{0:T(128)S(1)} collective-permute-done((f32[128]{0:T(128)S(1)}, f32[128]{0:T(128)S(1)}, u32[]{:S(2)}, u32[]{:S(2)}) %collective-permute-start.11) | collective-permute-done | bytes 544 | tf_op jit(solution)/shard_map/ppermute | solution.py:44
  167.2 0.1 copy.17
  167.3 5.6 %collective-permute-done.12 = f32[128]{0:T(128)S(1)} collective-permute-done((f32[128]{0:T(128)S(1)}, f32[128]{0:T(128)S(1)}, u32[]{:S(2)}, u32[]{:S(2)}) %collective-permute-start.12) | collective-permute-done | bytes 544 | tf_op jit(solution)/shard_map/ppermute | solution.py:44
  172.9 5.7 %collective-permute-done.13 = f32[128]{0:T(128)S(1)} collective-permute-done((f32[128]{0:T(128)S(1)}, f32[128]{0:T(128)S(1)}, u32[]{:S(2)}, u32[]{:S(2)}) %collective-permute-start.13) | collective-permute-done | bytes 544 | tf_op jit(solution)/shard_map/ppermute | solution.py:44
  178.7 5.5 %collective-permute-done.14 = f32[128]{0:T(128)S(1)} collective-permute-done((f32[128]{0:T(128)S(1)}, f32[128]{0:T(128)S(1)}, u32[]{:S(2)}, u32[]{:S(2)}) %collective-permute-start.14) | collective-permute-done | bytes 544 | tf_op jit(solution)/shard_map/ppermute | solution.py:44
  184.8 0.5 fusion.7
  185.2 0.4 fusion.6
  185.7 0.6 copy-done.1
  186.3 0.5 multiply_reduce_fusion
  186.8 2.3 fusion.5
  189.0 17.1 %all-gather.3 = f32[16,1,128]{2,1,0:T(1,128)S(1)} all-gather(f32[1,1,128]{2,1,0:T(1,128)S(1)} %bitcast.22), channel_id=1, replica_groups=mesh['grp'=2,'seq'=16] {'seq'}, dimensions={0}, use_global_device_ids=true | all-gather | bytes 8704 | tf_op jit(solution)/shard_map/all_gather | solution.py:138
  206.1 19.1 %all-gather.2 = f32[16,1,128]{2,1,0:T(1,128)S(1)} all-gather(f32[1,1,128]{2,1,0:T(1,128)S(1)} %bitcast.21), channel_id=1, replica_groups=mesh['grp'=2,'seq'=16] {'seq'}, dimensions={0}, use_global_device_ids=true | all-gather | bytes 8704 | tf_op jit(solution)/shard_map/all_gather | solution.py:137
  225.2 2.9 %fusion.19 = f32[128,128]{1,0:T(8,128)} fusion(bf16[2048,128]{1,0:T(8,128)(2,1)} %all_gather.33, f32[2048,128]{1,0:T(8,128)S(1)} %convolution_multiply_fusion, f32[2048]{0:T(1024)S(1)} %bitcast.19, f32[128]{0:T(128)S(1)} %add.199, f32[2048]{0:T(1024)S(1)} %dynamic_slice.38, s32[128]{0:T(128)S(1)} %add.196, s32[2048]{0:T(1024)S(1)} %add.192), kind=kOutput, calls=%fused_computation.27 | convolution fusion | flops 68681728 | bytes 1664000 | tf_op jit(solution)/shard_map/while/body/eval_jaxpr/dot_general | solution.py:17
  228.2 1.8 fusion.26
  230.0 0.1 reverse.4
  230.1 0.2 reduce_window_sum.18
  230.4 0.2 slice_reduce_fusion
  230.6 0.7 copy.18
  231.4 1.0 convolution_multiply_fusion.2
  232.3 0.2 dynamic-update-slice.2
  232.5 29.8 %all-reduce.2 = f32[32]{0:T(128)S(1)} all-reduce(f32[32]{0:T(128)S(1)} %dynamic-update-slice.2), channel_id=3, replica_groups=mesh['grp'=2,'seq'=16] {'seq'}, use_global_device_ids=true, to_apply=%add.2 | all-reduce | flops 32 | bytes 256
  262.3 0.2 fusion.22
  262.6 0.6 reshape.130
  (78 shorter events, 1.1 us)
Async XLA Ops:
  0.6 1.9 copy-start.6
  0.6 62.2 %copy-start.4 = (bf16[128,128]{1,0:T(8,128)(2,1)S(1)}, bf16[128,128]{1,0:T(8,128)(2,1)}, u32[]{:S(2)}) copy-start(bf16[128,128]{1,0:T(8,128)(2,1)} %param.6) | copy-start | bytes 98308
  40.0 42.4 %copy-start.2 = (bf16[128,128]{1,0:T(8,128)(2,1)S(1)}, bf16[128,128]{1,0:T(8,128)(2,1)}, u32[]{:S(2)}) copy-start(bf16[128,128]{1,0:T(8,128)(2,1)} %param.7) | copy-start | bytes 98308
  40.0 5.7 %collective-permute-start = (f32[128]{0:T(128)S(1)}, f32[128]{0:T(128)S(1)}, u32[]{:S(2)}, u32[]{:S(2)}) collective-permute-start(f32[128]{0:T(128)S(1)} %add.199), channel_id=1, source_target_pairs={{0,1},{1,2},{2,3},{3,4},{4,5},{5,6},{6,7},{7,8},{8,9},{9,10},{10,1... | collective-permute-start | bytes 1544 | tf_op jit(solution)/shard_map/ppermute | solution.py:44
  45.7 5.7 %collective-permute-start.1 = (f32[128]{0:T(128)S(1)}, f32[128]{0:T(128)S(1)}, u32[]{:S(2)}, u32[]{:S(2)}) collective-permute-start(f32[128]{0:T(128)S(1)} %collective-permute-done), channel_id=1, source_target_pairs={{0,1},{1,2},{2,3},{3,4},{4,5},{5,6},{6,7},{7,8},{8,9},{9,10},{10,1... | collective-permute-start | bytes 1544 | tf_op jit(solution)/shard_map/ppermute | solution.py:44
  51.4 5.7 %collective-permute-start.2 = (f32[128]{0:T(128)S(1)}, f32[128]{0:T(128)S(1)}, u32[]{:S(2)}, u32[]{:S(2)}) collective-permute-start(f32[128]{0:T(128)S(1)} %collective-permute-done.1), channel_id=1, source_target_pairs={{0,1},{1,2},{2,3},{3,4},{4,5},{5,6},{6,7},{7,8},{8,9},{9,10},{10,1... | collective-permute-start | bytes 1544 | tf_op jit(solution)/shard_map/ppermute | solution.py:44
  57.1 5.7 %collective-permute-start.3 = (f32[128]{0:T(128)S(1)}, f32[128]{0:T(128)S(1)}, u32[]{:S(2)}, u32[]{:S(2)}) collective-permute-start(f32[128]{0:T(128)S(1)} %collective-permute-done.2), channel_id=1, source_target_pairs={{0,1},{1,2},{2,3},{3,4},{4,5},{5,6},{6,7},{7,8},{8,9},{9,10},{10,1... | collective-permute-start | bytes 1544 | tf_op jit(solution)/shard_map/ppermute | solution.py:44
  62.8 19.4 %collective-permute-start.4 = (f32[128]{0:T(128)S(1)}, f32[128]{0:T(128)S(1)}, u32[]{:S(2)}, u32[]{:S(2)}) collective-permute-start(f32[128]{0:T(128)S(1)} %collective-permute-done.3), channel_id=1, source_target_pairs={{0,1},{1,2},{2,3},{3,4},{4,5},{5,6},{6,7},{7,8},{8,9},{9,10},{10,1... | collective-permute-start | bytes 1544 | tf_op jit(solution)/shard_map/ppermute | solution.py:44
  82.2 5.7 %collective-permute-start.5 = (f32[128]{0:T(128)S(1)}, f32[128]{0:T(128)S(1)}, u32[]{:S(2)}, u32[]{:S(2)}) collective-permute-start(f32[128]{0:T(128)S(1)} %collective-permute-done.4), channel_id=1, source_target_pairs={{0,1},{1,2},{2,3},{3,4},{4,5},{5,6},{6,7},{7,8},{8,9},{9,10},{10,1... | collective-permute-start | bytes 1544 | tf_op jit(solution)/shard_map/ppermute | solution.py:44
  82.7 24.8 %copy-start.5 = (bf16[128,128]{1,0:T(8,128)(2,1)S(1)}, bf16[128,128]{1,0:T(8,128)(2,1)}, u32[]{:S(2)}) copy-start(bf16[128,128]{1,0:T(8,128)(2,1)} %param.8) | copy-start | bytes 98308
  87.9 19.4 %collective-permute-start.6 = (f32[128]{0:T(128)S(1)}, f32[128]{0:T(128)S(1)}, u32[]{:S(2)}, u32[]{:S(2)}) collective-permute-start(f32[128]{0:T(128)S(1)} %collective-permute-done.5), channel_id=1, source_target_pairs={{0,1},{1,2},{2,3},{3,4},{4,5},{5,6},{6,7},{7,8},{8,9},{9,10},{10,1... | collective-permute-start | bytes 1544 | tf_op jit(solution)/shard_map/ppermute | solution.py:44
  107.3 22.3 %copy-start.3 = (bf16[128,128]{1,0:T(8,128)(2,1)S(1)}, bf16[128,128]{1,0:T(8,128)(2,1)}, u32[]{:S(2)}) copy-start(bf16[128,128]{1,0:T(8,128)(2,1)} %param.10) | copy-start | bytes 98308
  107.3 21.9 %collective-permute-start.7 = (f32[128]{0:T(128)S(1)}, f32[128]{0:T(128)S(1)}, u32[]{:S(2)}, u32[]{:S(2)}) collective-permute-start(f32[128]{0:T(128)S(1)} %collective-permute-done.6), channel_id=1, source_target_pairs={{0,1},{1,2},{2,3},{3,4},{4,5},{5,6},{6,7},{7,8},{8,9},{9,10},{10,1... | collective-permute-start | bytes 1544 | tf_op jit(solution)/shard_map/ppermute | solution.py:44
  129.3 20.8 %collective-permute-start.8 = (f32[128]{0:T(128)S(1)}, f32[128]{0:T(128)S(1)}, u32[]{:S(2)}, u32[]{:S(2)}) collective-permute-start(f32[128]{0:T(128)S(1)} %collective-permute-done.7), channel_id=1, source_target_pairs={{0,1},{1,2},{2,3},{3,4},{4,5},{5,6},{6,7},{7,8},{8,9},{9,10},{10,1... | collective-permute-start | bytes 1544 | tf_op jit(solution)/shard_map/ppermute | solution.py:44
  150.1 5.7 %collective-permute-start.9 = (f32[128]{0:T(128)S(1)}, f32[128]{0:T(128)S(1)}, u32[]{:S(2)}, u32[]{:S(2)}) collective-permute-start(f32[128]{0:T(128)S(1)} %collective-permute-done.8), channel_id=1, source_target_pairs={{0,1},{1,2},{2,3},{3,4},{4,5},{5,6},{6,7},{7,8},{8,9},{9,10},{10,1... | collective-permute-start | bytes 1544 | tf_op jit(solution)/shard_map/ppermute | solution.py:44
  155.8 5.7 %collective-permute-start.10 = (f32[128]{0:T(128)S(1)}, f32[128]{0:T(128)S(1)}, u32[]{:S(2)}, u32[]{:S(2)}) collective-permute-start(f32[128]{0:T(128)S(1)} %collective-permute-done.9), channel_id=1, source_target_pairs={{0,1},{1,2},{2,3},{3,4},{4,5},{5,6},{6,7},{7,8},{8,9},{9,10},{10,1... | collective-permute-start | bytes 1544 | tf_op jit(solution)/shard_map/ppermute | solution.py:44
  161.5 5.7 %collective-permute-start.11 = (f32[128]{0:T(128)S(1)}, f32[128]{0:T(128)S(1)}, u32[]{:S(2)}, u32[]{:S(2)}) collective-permute-start(f32[128]{0:T(128)S(1)} %collective-permute-done.10), channel_id=1, source_target_pairs={{0,1},{1,2},{2,3},{3,4},{4,5},{5,6},{6,7},{7,8},{8,9},{9,10},{10,1... | collective-permute-start | bytes 1544 | tf_op jit(solution)/shard_map/ppermute | solution.py:44
  167.2 5.7 %collective-permute-start.12 = (f32[128]{0:T(128)S(1)}, f32[128]{0:T(128)S(1)}, u32[]{:S(2)}, u32[]{:S(2)}) collective-permute-start(f32[128]{0:T(128)S(1)} %collective-permute-done.11), channel_id=1, source_target_pairs={{0,1},{1,2},{2,3},{3,4},{4,5},{5,6},{6,7},{7,8},{8,9},{9,10},{10,1... | collective-permute-start | bytes 1544 | tf_op jit(solution)/shard_map/ppermute | solution.py:44
  172.9 5.7 %collective-permute-start.13 = (f32[128]{0:T(128)S(1)}, f32[128]{0:T(128)S(1)}, u32[]{:S(2)}, u32[]{:S(2)}) collective-permute-start(f32[128]{0:T(128)S(1)} %collective-permute-done.12), channel_id=1, source_target_pairs={{0,1},{1,2},{2,3},{3,4},{4,5},{5,6},{6,7},{7,8},{8,9},{9,10},{10,1... | collective-permute-start | bytes 1544 | tf_op jit(solution)/shard_map/ppermute | solution.py:44
  178.6 5.7 %collective-permute-start.14 = (f32[128]{0:T(128)S(1)}, f32[128]{0:T(128)S(1)}, u32[]{:S(2)}, u32[]{:S(2)}) collective-permute-start(f32[128]{0:T(128)S(1)} %collective-permute-done.13), channel_id=1, source_target_pairs={{0,1},{1,2},{2,3},{3,4},{4,5},{5,6},{6,7},{7,8},{8,9},{9,10},{10,1... | collective-permute-start | bytes 1544 | tf_op jit(solution)/shard_map/ppermute | solution.py:44
  185.2 1.0 copy-start.1
  225.2 2.9 %copy-start = (bf16[2048,128]{1,0:T(8,128)(2,1)S(1)}, bf16[2048,128]{1,0:T(8,128)(2,1)}, u32[]{:S(2)}) copy-start(bf16[2048,128]{1,0:T(8,128)(2,1)} %all_gather.33) | copy-start | bytes 1572868
